TPU v7x, 32 devices: a whole 2x2x4 slice. The times are simulated.
32 devices in a mesh: groups: 2 (over x), seq: 8 (over z, y), head: 2 (over core).
Axes of the slice: x: 2, y: 2, z: 4, core: 2. Of those that a mesh axis runs over, the one named last changes fastest.
Arguments:
- query_rows: bfloat16 [2048, 6144], P(('groups', 'seq'), 'head'), parts along dimension 0
- key_rows: bfloat16 [2048, 6144], P(('groups', 'seq'), 'head'), parts along dimension 0, may hold values from -6 to 6
- value_rows: bfloat16 [2048, 6144], P(('groups', 'seq'), 'head'), parts along dimension 0, may hold values from -6 to 6
- key_len: int32 [16], P('groups'), parts along dimension 0, may hold values from 2 to 128, as said below
- linear_scale: float32 [48], P('head'), may hold values from 0.5 to 2
Outputs:
- attended: bfloat16 [2048, 6144], P(('groups', 'seq'), 'head'), parts along dimension 0
There are 2 independent parts, one for each index of `groups`. A program takes and returns all parts, laid end to end along the dimension named above; an argument that names none is the same for every part. Nothing has to cross between parts.
Inputs may be any that keep to these rules, and one draw needn't show every extreme that they name: `key_len`: one block has exactly 128 valid keys in every draw.
All inputs are finite; a program needn't handle non-finite values.
Results may differ from a plain program's by a relative error of at most 0.00135.
Values may be sent and summed in bfloat16 or wider, within the bound.
A program may use at most 256 MiB of HBM per device.

v0:
```python
import functools
import math

import jax
import jax.numpy as jnp
from jax import lax
from jax.experimental import pallas as pl
from jax.experimental.pallas import tpu as pltpu
from jax.sharding import PartitionSpec as P

HEADS_PER_CHUNK = 2
WINDOW = 3
LAG_TIMES = 5
LAG_OVER = 3


def feature(inputs):
    return jnp.where(inputs > 0.0, inputs + 1.0, jnp.exp(jnp.minimum(inputs, 0.0)))


def two_terms(wide):
    coarse = wide.astype(jnp.bfloat16)
    return coarse, (wide - coarse.astype(jnp.float32)).astype(jnp.bfloat16)


def kernel(
    blocks, heads, width, per_chunk, window, delay,
    len_ref, scale_ref, q_hbm, k_hbm, v_hbm, out_ref,
    q_ref, k_ref, v_ref, load_sem, far, acc, own_sums, near_sums, chain_out, chain_in, swap_in,
    send_sem, recv_sem, chain_send, chain_recv, swap_send, swap_recv,
):
    rows = q_ref.shape[0]
    levels = blocks.bit_length() - 1
    chunks = heads // per_chunk
    half = chunks // 2
    pairs = blocks // 2
    span = per_chunk * width
    linear_lag = max(half, delay(pairs - 1) + 1)
    linear_first = linear_lag == half
    turns = max(chunks, half + linear_lag)

    me = lax.axis_index("seq")
    side = lax.rem(me, 2)
    pair = me // 2
    partners = [me + (1 - 2 * lax.rem(me // (1 << bit), 2)) * (1 << bit) for bit in range(levels)]
    above = lax.rem(me + 2, blocks)
    below = lax.rem(me + blocks - 2, blocks)

    def place(turn, which):
        return lax.rem(turn + half * which, chunks)

    def columns(chunk):
        return pl.ds(pl.multiple_of(chunk * span, span), span)

    def block_copy(bit, turn, part, which):
        source = k_hbm if part == 0 else v_hbm
        cut = columns(place(turn, which))
        return pltpu.make_async_remote_copy(
            src_ref=source.at[:, cut],
            dst_ref=far.at[bit, part, :, cut],
            send_sem=send_sem.at[bit, turn, part],
            recv_sem=recv_sem.at[bit, turn, part],
            device_id={"seq": partners[bit]},
            device_id_type=pl.DeviceIdType.MESH,
        )

    def chain_copy(turn):
        return pltpu.make_async_remote_copy(
            src_ref=chain_out.at[turn],
            dst_ref=chain_in.at[turn],
            send_sem=chain_send.at[turn],
            recv_sem=chain_recv.at[turn],
            device_id={"seq": above},
            device_id_type=pl.DeviceIdType.MESH,
        )

    def swap_copy(turn):
        return pltpu.make_async_remote_copy(
            src_ref=chain_in.at[turn],
            dst_ref=swap_in.at[turn],
            send_sem=swap_send.at[turn],
            recv_sem=swap_recv.at[turn],
            device_id={"seq": partners[0]},
            device_id_type=pl.DeviceIdType.MESH,
        )

    loads = [
        pltpu.make_async_copy(source, target, load_sem.at[index])
        for index, (source, target) in enumerate(((k_hbm, k_ref), (v_hbm, v_ref), (q_hbm, q_ref)))
    ]
    barrier = pltpu.get_barrier_semaphore()
    greeted = partners + [above, below]
    for other in greeted:
        pl.semaphore_signal(
            barrier, inc=1, device_id={"seq": other}, device_id_type=pl.DeviceIdType.MESH
        )
    pl.semaphore_wait(barrier, len(greeted))

    def send_far(turn):
        for bit in range(1, levels):
            for part in range(2):
                block_copy(bit, turn, part, side).start()

    def send_near(turn, _):
        for part in range(2):
            block_copy(0, turn, part, 1 - side).start()
        return 0

    lax.fori_loop(0, min(window, chunks), lambda turn, _: (send_far(turn), 0)[1], 0)
    lax.fori_loop(0, chunks, send_near, 0)

    for load in loads:
        load.start()

    row_ids = lax.broadcasted_iota(jnp.int32, (rows, rows), 0)
    column_ids = lax.broadcasted_iota(jnp.int32, (rows, rows), 1)
    live_rows = lax.broadcasted_iota(jnp.int32, (rows, width), 0)
    root = 1.0 / math.sqrt(width)
    lengths = [len_ref[me]] + [len_ref[partner] for partner in partners]

    def head_columns(head):
        return pl.ds(pl.multiple_of(head * width, width), width)

    def key_value_sum(keys, values, length):
        mapped = jnp.where(live_rows < length, feature(keys.astype(jnp.float32)), 0.0)
        return sum(
            lax.dot_general(
                term, values, (((0,), (0,)), ((), ())), preferred_element_type=jnp.float32
            )
            for term in two_terms(mapped)
        )

    def attend(head, finishing):
        cut = head_columns(head)
        queries = q_ref[:, cut]
        pieces = []
        for index in range(levels + 1):
            if index == 0:
                keys, values = k_ref[:, cut], v_ref[:, cut]
            else:
                keys, values = far[index - 1, 0, :, cut], far[index - 1, 1, :, cut]
            scores = root * lax.dot_general(
                queries, keys, (((1,), (1,)), ((), ())), preferred_element_type=jnp.float32
            )
            allowed = column_ids < lengths[index]
            if index == 0:
                allowed = allowed & (column_ids <= row_ids)
            peak = jnp.max(jnp.where(allowed, scores, -jnp.inf), axis=1, keepdims=True)
            weights = jnp.where(allowed, jnp.exp(scores - peak), 0.0).astype(jnp.bfloat16)
            total = jnp.sum(weights.astype(jnp.float32), axis=1, keepdims=True)
            numerator = jnp.dot(weights, values, preferred_element_type=jnp.float32)
            pieces.append((numerator, peak, total))
        top = functools.reduce(jnp.maximum, [peak for _, peak, _ in pieces])
        numerator, denominator = 0.0, 0.0
        for piece, peak, total in pieces:
            factor = jnp.exp(peak - top)
            numerator = numerator + factor * piece
            denominator = denominator + factor * total
        attention = numerator / denominator
        if finishing:
            out_ref[:, cut] = (attention + acc[:, cut]).astype(out_ref.dtype)
        else:
            acc[:, cut] = attention

    def add_linear(head, prefix, finishing):
        cut = head_columns(head)
        near = jnp.where(side > 0, near_sums[head], 0.0)
        prefix = jnp.where(pair > 0, prefix.astype(jnp.float32), 0.0) + near
        coarse, fine = two_terms(feature(q_ref[:, cut].astype(jnp.float32)))
        sums, rest = two_terms(prefix)
        linear = sum(
            jnp.dot(left, right, preferred_element_type=jnp.float32)
            for left, right in ((coarse, sums), (fine, sums), (coarse, rest))
        )
        gain = scale_ref[head] / (width * math.sqrt(rows * blocks))
        linear = gain * linear
        if finishing:
            out_ref[:, cut] = (acc[:, cut] + linear).astype(out_ref.dtype)
        else:
            acc[:, cut] = linear

    def one_turn(turn, _):
        @pl.when(turn < chunks)
        def _():
            chunk = place(turn, side)
            for part in range(2):
                block_copy(0, turn, part, side).wait_recv()
            for offset in range(per_chunk):
                head = chunk * per_chunk + offset
                cut = head_columns(head)
                near_sums[head] = key_value_sum(far[0, 0, :, cut], far[0, 1, :, cut], lengths[1])

            @pl.when(turn < half)
            def _():
                for offset in range(per_chunk):
                    cut = head_columns(chunk * per_chunk + offset)
                    own_sums[turn * per_chunk + offset] = key_value_sum(
                        k_ref[:, cut], v_ref[:, cut], lengths[0]
                    )

        link = turn - delay(pair)

        @pl.when((link >= 0) & (link < half))
        def _():
            first = place(link, side) * per_chunk

            @pl.when(pair > 0)
            def _():
                chain_copy(link).wait_recv()
                swap_copy(link).start()

            @pl.when(pair < pairs - 1)
            def _():
                for offset in range(per_chunk):
                    both = own_sums[link * per_chunk + offset] + near_sums[first + offset]
                    before = jnp.where(pair > 0, chain_in[link, offset].astype(jnp.float32), 0.0)
                    chain_out[link, offset] = (both + before).astype(jnp.bfloat16)
                chain_copy(link).start()

        @pl.when(turn + window < chunks)
        def _():
            send_far(turn + window)

        late = turn - linear_lag

        @pl.when((late >= 0) & (late < half))
        def _():
            @pl.when(pair > 0)
            def _():
                swap_copy(late).wait_recv()

            for offset in range(per_chunk):
                add_linear(place(late, side) * per_chunk + offset, chain_in[late, offset], True)
                add_linear(place(late, 1 - side) * per_chunk + offset, swap_in[late, offset], not linear_first)

        def attend_chunk(finishing):
            chunk = place(turn, side)
            for bit in range(1, levels):
                for part in range(2):
                    block_copy(bit, turn, part, side).wait_recv()
            for offset in range(per_chunk):
                attend(chunk * per_chunk + offset, finishing)

        pl.when(turn < half)(lambda: attend_chunk(False))
        pl.when((turn >= half) & (turn < chunks))(lambda: attend_chunk(linear_first))

        return 0

    @pl.when(pair == 0)
    def _():
        def clear(turn, _):
            chain_in[turn] = jnp.zeros_like(chain_in[turn])
            swap_in[turn] = jnp.zeros_like(swap_in[turn])
            return 0

        lax.fori_loop(0, half, clear, 0)

    for load in loads:
        load.wait()

    lax.fori_loop(0, turns, one_turn, 0)

    def finish(turn, _):
        for part in range(2):
            block_copy(0, turn, part, 1 - side).wait_send()
            for bit in range(1, levels):
                block_copy(bit, turn, part, side).wait_send()
        return 0

    lax.fori_loop(0, chunks, finish, 0)

    def finish_chain(turn, _):
        @pl.when(pair < pairs - 1)
        def _():
            chain_copy(turn).wait_send()

        @pl.when(pair > 0)
        def _():
            swap_copy(turn).wait_send()

        return 0

    lax.fori_loop(0, half, finish_chain, 0)


def delay(pair):
    return (LAG_TIMES * pair + 1) // LAG_OVER


def shards(blocks, query_rows, key_rows, value_rows, key_len, linear_scale):
    rows, total = query_rows.shape
    heads = linear_scale.shape[0]
    width = total // heads
    levels = blocks.bit_length() - 1
    chunks = heads // HEADS_PER_CHUNK
    half = chunks // 2
    vmem = pl.BlockSpec(memory_space=pltpu.VMEM)
    hbm = pl.BlockSpec(memory_space=pltpu.HBM)
    smem = pl.BlockSpec(memory_space=pltpu.SMEM)
    piece = (half, HEADS_PER_CHUNK, width, width)
    dma = pltpu.SemaphoreType.DMA
    return pl.pallas_call(
        functools.partial(kernel, blocks, heads, width, HEADS_PER_CHUNK, WINDOW, delay),
        out_shape=jax.ShapeDtypeStruct((rows, total), query_rows.dtype),
        in_specs=[smem, smem, hbm, hbm, hbm],
        out_specs=vmem,
        scratch_shapes=[
            pltpu.VMEM((rows, total), jnp.bfloat16),
            pltpu.VMEM((rows, total), jnp.bfloat16),
            pltpu.VMEM((rows, total), jnp.bfloat16),
            dma((3,)),
            pltpu.VMEM((levels, 2, rows, total), jnp.bfloat16),
            pltpu.VMEM((rows, total), jnp.float32),
            pltpu.VMEM((heads // 2, width, width), jnp.float32),
            pltpu.VMEM((heads, width, width), jnp.float32),
            pltpu.VMEM(piece, jnp.bfloat16),
            pltpu.VMEM(piece, jnp.bfloat16),
            pltpu.VMEM(piece, jnp.bfloat16),
            dma((levels, chunks, 2)),
            dma((levels, chunks, 2)),
            dma((half,)),
            dma((half,)),
            dma((half,)),
            dma((half,)),
        ],
        compiler_params=pltpu.CompilerParams(
            collective_id=0, has_side_effects=True, vmem_limit_bytes=55000000
        ),
        name="butterfly",
    )(key_len, linear_scale, query_rows, key_rows, value_rows)


def solution(mesh):
    return jax.shard_map(
        functools.partial(shards, mesh.shape["seq"]),
        mesh=mesh,
        in_specs=(
            P(("groups", "seq"), "head"),
            P(("groups", "seq"), "head"),
            P(("groups", "seq"), "head"),
            P("groups"),
            P("head"),
        ),
        out_specs=P(("groups", "seq"), "head"),
        check_vma=False,
    )
```

profile of v0, /device:TPU:0, one launch (start us, length us, event | category | flops | bytes accessed | tf_op | source)
XLA Modules:
  0.0 85.5 jit_solution(2071124573111884274)
XLA Ops:
  0.0 0.0 copy-start
  0.0 0.7 copy-done
  0.7 0.0 copy-start.1
  0.7 0.7 copy-done.1
  1.3 83.3 %butterfly.1 = bf16[128,3072]{1,0:T(8,128)(2,1)S(1)} custom-call(s32[8]{0:T(128)S(1)} %copy-done, f32[24]{0:T(128)S(1)} %copy-done.1, bf16[128,3072]{1,0:T(8,128)(2,1)} %q_hbm.1, bf16[128,3072]{1,0:T(8,128)(2,1)} %k_hbm.1, bf16[128,3072]{1,0:T(8,128)(2,1)} %v_hbm.1), custom_call_target="tpu_custom_call" | custom-call | tf_op jit(solution)/shard_map/butterfly/pallas_call | solution.py:302
  84.6 0.9 %copy.7 = bf16[128,3072]{1,0:T(8,128)(2,1)} copy(bf16[128,3072]{1,0:T(8,128)(2,1)S(1)} %butterfly.1) | data formatting | bytes 1572864
Async XLA Ops:
  0.0 0.7 copy-start
  0.7 0.7 copy-start.1
where the time goes:
time: 87.2 us; the launch traced here: 85.5 us
  Pallas kernels  83.3 us (96%)
  local copies, waits for them, and re-layouts  2.19 us (3%)
    pallas_call x1, Pallas kernels, shards(): pl.pallas_call(functools.partial(kernel, blocks, heads, width, HEADS_PER_...  83.3 us
    unnamed x5, local copies, waits for them, and re-layouts  2.19 us

commit v1 on v0

--- a/solution.py
+++ b/solution.py
@@ -24,10 +24,11 @@
 
 
 def kernel(
-    blocks, heads, width, per_chunk, window, delay,
-    len_ref, scale_ref, q_hbm, k_hbm, v_hbm, out_ref,
-    q_ref, k_ref, v_ref, load_sem, far, acc, own_sums, near_sums, chain_out, chain_in, swap_in,
+    blocks, heads, width, per_chunk, window, delay, serve,
+    len_hbm, scale_hbm, q_hbm, k_hbm, v_hbm, out_ref,
+    len_ref, scale_ref, q_ref, k_ref, v_ref, load_sem, far, acc, own_sums, near_sums, chain_out, chain_in, swap_in,
     send_sem, recv_sem, chain_send, chain_recv, swap_send, swap_recv,
+    guest_q, served_out, served_in, stats_out, stats_in, ask_send, ask_recv, answer_send, answer_recv,
 ):
     rows = q_ref.shape[0]
     levels = blocks.bit_length() - 1
@@ -60,7 +61,7 @@
             dst_ref=far.at[bit, part, :, cut],
             send_sem=send_sem.at[bit, turn, part],
             recv_sem=recv_sem.at[bit, turn, part],
-            device_id={"seq": partners[bit]},
+            device_id={"seq": partners[bit] if isinstance(bit, int) else partners[1]},
             device_id_type=pl.DeviceIdType.MESH,
         )
 
@@ -84,10 +85,55 @@
             device_id_type=pl.DeviceIdType.MESH,
         )
 
+    host = jnp.where(pair == 1, below, partners[-1])
+    guest = jnp.where(pair == 0, above, partners[-1])
+
+    def served(turn):
+        return (turn >= half) & (lax.rem(turn, 2) == 1) if serve else False
+
+    def served_turn(index):
+        return half + 1 - half % 2 + 2 * index
+
+    def served_index(turn):
+        return (turn - half) // 2
+
+    def withheld(bit, turn):
+        return served(turn) & (pair == bit - 1)
+
+    def answered(bit, turn):
+        return served(turn) & (pair == 2 * bit - 1)
+
+    def ask_copy(index):
+        return pltpu.make_async_remote_copy(
+            src_ref=q_hbm.at[:, columns(place(served_turn(index), side))],
+            dst_ref=guest_q.at[index],
+            send_sem=ask_send.at[index],
+            recv_sem=ask_recv.at[index],
+            device_id={"seq": host},
+            device_id_type=pl.DeviceIdType.MESH,
+        )
+
+    def answer_copies(index):
+        return [
+            pltpu.make_async_remote_copy(
+                src_ref=source.at[index],
+                dst_ref=target.at[index],
+                send_sem=answer_send.at[index, part],
+                recv_sem=answer_recv.at[index, part],
+                device_id={"seq": guest},
+                device_id_type=pl.DeviceIdType.MESH,
+            )
+            for part, (source, target) in enumerate(((served_out, served_in), (stats_out, stats_in)))
+        ]
+
     loads = [
         pltpu.make_async_copy(source, target, load_sem.at[index])
-        for index, (source, target) in enumerate(((k_hbm, k_ref), (v_hbm, v_ref), (q_hbm, q_ref)))
+        for index, (source, target) in enumerate(
+            ((k_hbm, k_ref), (v_hbm, v_ref), (q_hbm, q_ref), (len_hbm, len_ref), (scale_hbm, scale_ref))
+        )
     ]
+    for load in loads:
+        load.start()
     barrier = pltpu.get_barrier_semaphore()
     greeted = partners + [above, below]
     for other in greeted:
@@ -96,26 +142,41 @@
         )
     pl.semaphore_wait(barrier, len(greeted))
 
+    def unless(condition, action):
+        if condition is False:
+            action()
+        else:
+            pl.when(jnp.logical_not(condition))(action)
+
     def send_far(turn):
         for bit in range(1, levels):
-            for part in range(2):
-                block_copy(bit, turn, part, side).start()
+            def start(bit=bit):
+                for part in range(2):
+                    block_copy(bit, turn, part, side).start()
+
+            unless(withheld(bit, turn) if serve else False, start)
 
     def send_near(turn, _):
         for part in range(2):
             block_copy(0, turn, part, 1 - side).start()
         return 0
 
+    if serve:
+        @pl.when(lax.rem(pair, 2) == 1)
+        def _():
+            for index in range(serve):
+                ask_copy(index).start()
+
     lax.fori_loop(0, min(window, chunks), lambda turn, _: (send_far(turn), 0)[1], 0)
     lax.fori_loop(0, chunks, send_near, 0)
-
-    for load in loads:
-        load.start()
 
     row_ids = lax.broadcasted_iota(jnp.int32, (rows, rows), 0)
     column_ids = lax.broadcasted_iota(jnp.int32, (rows, rows), 1)
     live_rows = lax.broadcasted_iota(jnp.int32, (rows, width), 0)
     root = 1.0 / math.sqrt(width)
+
+    for load in loads:
+        load.wait()
     lengths = [len_ref[me]] + [len_ref[partner] for partner in partners]
 
     def head_columns(head):
@@ -130,37 +191,80 @@
             for term in two_terms(mapped)
         )
 
-    def attend(head, finishing):
-        cut = head_columns(head)
-        queries = q_ref[:, cut]
-        pieces = []
-        for index in range(levels + 1):
-            if index == 0:
-                keys, values = k_ref[:, cut], v_ref[:, cut]
-            else:
-                keys, values = far[index - 1, 0, :, cut], far[index - 1, 1, :, cut]
-            scores = root * lax.dot_general(
-                queries, keys, (((1,), (1,)), ((), ())), preferred_element_type=jnp.float32
-            )
-            allowed = column_ids < lengths[index]
-            if index == 0:
-                allowed = allowed & (column_ids <= row_ids)
-            peak = jnp.max(jnp.where(allowed, scores, -jnp.inf), axis=1, keepdims=True)
-            weights = jnp.where(allowed, jnp.exp(scores - peak), 0.0).astype(jnp.bfloat16)
-            total = jnp.sum(weights.astype(jnp.float32), axis=1, keepdims=True)
-            numerator = jnp.dot(weights, values, preferred_element_type=jnp.float32)
-            pieces.append((numerator, peak, total))
+    def piece(queries, keys, values, length, causal):
+        scores = root * lax.dot_general(
+            queries, keys, (((1,), (1,)), ((), ())), preferred_element_type=jnp.float32
+        )
+        allowed = column_ids < length
+        if causal:
+            allowed = allowed & (column_ids <= row_ids)
+        peak = jnp.max(jnp.where(allowed, scores, -jnp.inf), axis=1, keepdims=True)
+        weights = jnp.where(allowed, jnp.exp(scores - peak), 0.0).astype(jnp.bfloat16)
+        total = jnp.sum(weights.astype(jnp.float32), axis=1, keepdims=True)
+        numerator = jnp.dot(weights, values, preferred_element_type=jnp.float32)
+        return numerator, peak, total
+
+    def merge(pieces):
         top = functools.reduce(jnp.maximum, [peak for _, peak, _ in pieces])
         numerator, denominator = 0.0, 0.0
-        for piece, peak, total in pieces:
+        for part, peak, total in pieces:
             factor = jnp.exp(peak - top)
-            numerator = numerator + factor * piece
+            numerator = numerator + factor * part
             denominator = denominator + factor * total
-        attention = numerator / denominator
-        if finishing:
-            out_ref[:, cut] = (attention + acc[:, cut]).astype(out_ref.dtype)
+        return numerator / denominator
+
+    def attend(turn, finishing, asked):
+        chunk = place(turn, side)
+        cuts = [head_columns(chunk * per_chunk + offset) for offset in range(per_chunk)]
+        pieces = [
+            [
+                piece(q_ref[:, cut], k_ref[:, cut], v_ref[:, cut], lengths[0], True),
+                piece(q_ref[:, cut], far[0, 0, :, cut], far[0, 1, :, cut], lengths[1], False),
+            ]
+            for cut in cuts
+        ]
+        if asked:
+            index = served_index(turn)
+            for copy in answer_copies(index):
+                copy.wait_recv()
+            columns_of = jnp.tile(stats_in[index], (rows // 8, 1)).T
+            for offset, found in enumerate(pieces):
+                part = served_in[index, :, offset * width:(offset + 1) * width].astype(jnp.float32)
+                at = 2 * offset
+                found.append((part, columns_of[:, at:at + 1], columns_of[:, at + 1:at + 2]))
+            remaining = [jnp.where(pair == 1, 2, 1)]
+            extents = [jnp.where(pair == 1, lengths[3], lengths[2])]
         else:
-            acc[:, cut] = attention
+            remaining = range(1, levels)
+            extents = lengths[2:]
+        for bit, extent in zip(remaining, extents):
+            for part in range(2):
+                block_copy(bit, turn, part, side).wait_recv()
+            for cut, found in zip(cuts, pieces):
+                found.append(piece(q_ref[:, cut], far[bit, 0, :, cut], far[bit, 1, :, cut], extent, False))
+        for cut, found in zip(cuts, pieces):
+            attention = merge(found)
+            if finishing:
+                out_ref[:, cut] = (attention + acc[:, cut]).astype(out_ref.dtype)
+            else:
+                acc[:, cut] = attention
+
+    def answer(index):
+        ask_copy(index).wait_recv()
+        chunk = place(served_turn(index), side)
+        lanes = jnp.zeros((rows, rows), jnp.float32)
+        for offset in range(per_chunk):
+            cut = head_columns(chunk * per_chunk + offset)
+            local = slice(offset * width, (offset + 1) * width)
+            numerator, peak, total = piece(
+                guest_q[index, :, local], k_ref[:, cut], v_ref[:, cut], lengths[0], False
+            )
+            served_out[index, :, local] = numerator.astype(jnp.bfloat16)
+            lanes = jnp.where(column_ids == 2 * offset, peak, lanes)
+            lanes = jnp.where(column_ids == 2 * offset + 1, total, lanes)
+        stats_out[index] = lanes.T[:8]
+        for copy in answer_copies(index):
+            copy.start()
 
     def add_linear(head, prefix, finishing):
         cut = head_columns(head)
@@ -233,16 +337,19 @@
                 add_linear(place(late, side) * per_chunk + offset, chain_in[late, offset], True)
                 add_linear(place(late, 1 - side) * per_chunk + offset, swap_in[late, offset], not linear_first)
 
-        def attend_chunk(finishing):
-            chunk = place(turn, side)
-            for bit in range(1, levels):
-                for part in range(2):
-                    block_copy(bit, turn, part, side).wait_recv()
-            for offset in range(per_chunk):
-                attend(chunk * per_chunk + offset, finishing)
-
-        pl.when(turn < half)(lambda: attend_chunk(False))
-        pl.when((turn >= half) & (turn < chunks))(lambda: attend_chunk(linear_first))
+        if serve:
+            @pl.when((pair < pairs // 2) & (lax.rem(turn, 2) == 1) & (turn // 2 < serve))
+            def _():
+                answer(turn // 2)
+
+        asking = served(turn) & (lax.rem(pair, 2) == 1)
+        second = (turn >= half) & (turn < chunks)
+        pl.when(turn < half)(lambda: attend(turn, False, False))
+        if serve:
+            pl.when(second & jnp.logical_not(asking))(lambda: attend(turn, linear_first, False))
+            pl.when(second & asking)(lambda: attend(turn, linear_first, True))
+        else:
+            pl.when(second)(lambda: attend(turn, linear_first, False))
 
         return 0
 
@@ -255,16 +362,17 @@
 
         lax.fori_loop(0, half, clear, 0)
 
-    for load in loads:
-        load.wait()
-
     lax.fori_loop(0, turns, one_turn, 0)
 
     def finish(turn, _):
         for part in range(2):
             block_copy(0, turn, part, 1 - side).wait_send()
-            for bit in range(1, levels):
-                block_copy(bit, turn, part, side).wait_send()
+        for bit in range(1, levels):
+            def wait(bit=bit):
+                for part in range(2):
+                    block_copy(bit, turn, part, side).wait_send()
+
+            unless(withheld(bit, turn) if serve else False, wait)
         return 0
 
     lax.fori_loop(0, chunks, finish, 0)
@@ -281,6 +389,20 @@
         return 0
 
     lax.fori_loop(0, half, finish_chain, 0)
+
+    def finish_served(index, _):
+        @pl.when(lax.rem(pair, 2) == 1)
+        def _():
+            ask_copy(index).wait_send()
+
+        @pl.when(pair < pairs // 2)
+        def _():
+            for copy in answer_copies(index):
+                copy.wait_send()
+
+        return 0
+
+    lax.fori_loop(0, serve, finish_served, 0)
 
 
 def delay(pair):
@@ -294,21 +416,25 @@
     levels = blocks.bit_length() - 1
     chunks = heads // HEADS_PER_CHUNK
     half = chunks // 2
+    serve = half // 2 if blocks == 8 else 0
+    guests = max(serve, 1)
+    span = HEADS_PER_CHUNK * width
     vmem = pl.BlockSpec(memory_space=pltpu.VMEM)
     hbm = pl.BlockSpec(memory_space=pltpu.HBM)
-    smem = pl.BlockSpec(memory_space=pltpu.SMEM)
     piece = (half, HEADS_PER_CHUNK, width, width)
     dma = pltpu.SemaphoreType.DMA
     return pl.pallas_call(
-        functools.partial(kernel, blocks, heads, width, HEADS_PER_CHUNK, WINDOW, delay),
+        functools.partial(kernel, blocks, heads, width, HEADS_PER_CHUNK, WINDOW, delay, serve),
         out_shape=jax.ShapeDtypeStruct((rows, total), query_rows.dtype),
-        in_specs=[smem, smem, hbm, hbm, hbm],
+        in_specs=[hbm, hbm, hbm, hbm, hbm],
         out_specs=vmem,
         scratch_shapes=[
+            pltpu.SMEM((blocks,), jnp.int32),
+            pltpu.SMEM((heads,), jnp.float32),
             pltpu.VMEM((rows, total), jnp.bfloat16),
             pltpu.VMEM((rows, total), jnp.bfloat16),
             pltpu.VMEM((rows, total), jnp.bfloat16),
-            dma((3,)),
+            dma((5,)),
             pltpu.VMEM((levels, 2, rows, total), jnp.bfloat16),
             pltpu.VMEM((rows, total), jnp.float32),
             pltpu.VMEM((heads // 2, width, width), jnp.float32),
@@ -322,6 +448,15 @@
             dma((half,)),
             dma((half,)),
             dma((half,)),
+            pltpu.VMEM((guests, rows, span), jnp.bfloat16),
+            pltpu.VMEM((guests, rows, span), jnp.bfloat16),
+            pltpu.VMEM((guests, rows, span), jnp.bfloat16),
+            pltpu.VMEM((guests, 8, rows), jnp.float32),
+            pltpu.VMEM((guests, 8, rows), jnp.float32),
+            dma((guests,)),
+            dma((guests,)),
+            dma((guests, 2)),
+            dma((guests, 2)),
         ],
         compiler_params=pltpu.CompilerParams(
             collective_id=0, has_side_effects=True, vmem_limit_bytes=55000000

time: 87.2 us -> 83.8 us (0.961); the launches traced: 85.5 us -> 83.3 us
  Pallas kernels: 83.3 us -> 81.1 us
    pallas_call x1, Pallas kernels: 83.3 us -> 81.1 us  [shards(): pl.pallas_call(functools.partial(kernel, blocks, heads, width, HEADS_PER_...]
where the time goes in v1:
time: 83.8 us; the launch traced here: 83.3 us
  Pallas kernels  81.1 us (97%)
  local copies, waits for them, and re-layouts  2.19 us (3%)
    pallas_call x1, Pallas kernels, shards(): pl.pallas_call(functools.partial(kernel, blocks, heads, width, HEADS_PER_...  81.1 us
    unnamed x5, local copies, waits for them, and re-layouts  2.19 us

profile of v1, /device:TPU:0, one launch (start us, length us, event | category | flops | bytes accessed | tf_op | source)
XLA Modules:
  0.0 83.3 jit_solution(18035576662202311948)
XLA Ops:
  0.0 0.0 copy-start
  0.0 0.7 copy-done
  0.7 0.0 copy-start.1
  0.7 0.7 copy-done.1
  1.3 81.1 %butterfly.1 = bf16[128,3072]{1,0:T(8,128)(2,1)S(1)} custom-call(s32[8]{0:T(128)S(1)} %copy-done, f32[24]{0:T(128)S(1)} %copy-done.1, bf16[128,3072]{1,0:T(8,128)(2,1)} %q_hbm.1, bf16[128,3072]{1,0:T(8,128)(2,1)} %k_hbm.1, bf16[128,3072]{1,0:T(8,128)(2,1)} %v_hbm.1), custom_call_target="tpu_custom_call" | custom-call | tf_op jit(solution)/shard_map/butterfly/pallas_call | solution.py:426
  82.4 0.9 %copy.7 = bf16[128,3072]{1,0:T(8,128)(2,1)} copy(bf16[128,3072]{1,0:T(8,128)(2,1)S(1)} %butterfly.1) | data formatting | bytes 1572864
Async XLA Ops:
  0.0 0.7 copy-start
  0.7 0.7 copy-start.1

commit v2 on v1

--- a/solution.py
+++ b/solution.py
@@ -462,7 +462,11 @@
             collective_id=0, has_side_effects=True, vmem_limit_bytes=55000000
         ),
         name="butterfly",
-    )(key_len, linear_scale, query_rows, key_rows, value_rows)
+    )(
+        pltpu.with_memory_space_constraint(key_len, pltpu.HBM),
+        pltpu.with_memory_space_constraint(linear_scale, pltpu.HBM),
+        query_rows, key_rows, value_rows,
+    )
 
 
 def solution(mesh):

time: 83.8 us -> 82.4 us (0.983)
  local copies, waits for them, and re-layouts: 2.19 us -> 0.88 us
    unnamed x5 -> x1, local copies, waits for them, and re-layouts: 2.19 us -> 0.88 us
where the time goes in v2:
time: 82.4 us; the launch traced here: 82 us
  Pallas kernels  81.1 us (98%)
  local copies, waits for them, and re-layouts  0.88 us (1%)
    pallas_call x1, Pallas kernels, shards(): pl.pallas_call(functools.partial(kernel, blocks, heads, width, HEADS_PER_...  81.1 us

profile of v2, /device:TPU:0, one launch (start us, length us, event | category | flops | bytes accessed | tf_op | source)
XLA Modules:
  0.0 82.0 jit_solution(14069880457464893170)
XLA Ops:
  0.0 81.1 %butterfly.1 = bf16[128,3072]{1,0:T(8,128)(2,1)S(1)} custom-call(s32[8]{0:T(128)} %len_hbm.1, f32[24]{0:T(128)} %scale_hbm.1, bf16[128,3072]{1,0:T(8,128)(2,1)} %q_hbm.1, bf16[128,3072]{1,0:T(8,128)(2,1)} %k_hbm.1, bf16[128,3072]{1,0:T(8,128)(2,1)} %v_hbm.1), custom_call_target="tpu_custom_call" | custom-call | tf_op jit(solution)/shard_map/butterfly/pallas_call | solution.py:426
  81.1 0.9 %copy.7 = bf16[128,3072]{1,0:T(8,128)(2,1)} copy(bf16[128,3072]{1,0:T(8,128)(2,1)S(1)} %butterfly.1) | data formatting | bytes 1572864

commit v3 on v2

--- a/solution.py
+++ b/solution.py
@@ -9,8 +9,11 @@
 from jax.sharding import PartitionSpec as P
 
 HEADS_PER_CHUNK = 2
-WINDOW = 3
-LAG_TIMES = 5
+WINDOW = 2
+STEPS = 2
+CALM = 3
+SERVED = 5
+LAG_TIMES = 6
 LAG_OVER = 3
 
 
@@ -24,7 +27,7 @@
 
 
 def kernel(
-    blocks, heads, width, per_chunk, window, delay, serve,
+    blocks, heads, width, per_chunk, window, calm, delay, serve,
     len_hbm, scale_hbm, q_hbm, k_hbm, v_hbm, out_ref,
     len_ref, scale_ref, q_ref, k_ref, v_ref, load_sem, far, acc, own_sums, near_sums, chain_out, chain_in, swap_in,
     send_sem, recv_sem, chain_send, chain_recv, swap_send, swap_recv,
@@ -36,9 +39,10 @@
     half = chunks // 2
     pairs = blocks // 2
     span = per_chunk * width
-    linear_lag = max(half, delay(pairs - 1) + 1)
-    linear_first = linear_lag == half
-    turns = max(chunks, half + linear_lag)
+    rounds = pl.cdiv(half, STEPS)
+    linear_lag = max(chunks - rounds, delay(pairs - 1) + 1)
+    joined = linear_lag + rounds == chunks
+    turns = linear_lag + rounds
 
     me = lax.axis_index("seq")
     side = lax.rem(me, 2)
@@ -53,9 +57,12 @@
     def columns(chunk):
         return pl.ds(pl.multiple_of(chunk * span, span), span)
 
-    def block_copy(bit, turn, part, which):
+    def head_columns(head):
+        return pl.ds(pl.multiple_of(head * width, width), width)
+
+    def block_copy(bit, turn, part, which, heads_sent=per_chunk):
         source = k_hbm if part == 0 else v_hbm
-        cut = columns(place(turn, which))
+        cut = pl.ds(pl.multiple_of(place(turn, which) * span, span), heads_sent * width)
         return pltpu.make_async_remote_copy(
             src_ref=source.at[:, cut],
             dst_ref=far.at[bit, part, :, cut],
@@ -89,23 +96,20 @@
     guest = jnp.where(pair == 0, above, partners[-1])
 
     def served(turn):
-        return (turn >= half) & (lax.rem(turn, 2) == 1) if serve else False
+        return (turn >= chunks - serve) & (turn < chunks) if serve else False
 
     def served_turn(index):
-        return half + 1 - half % 2 + 2 * index
+        return chunks - serve + index
 
     def served_index(turn):
-        return (turn - half) // 2
+        return turn - (chunks - serve)
 
     def withheld(bit, turn):
         return served(turn) & (pair == bit - 1)
 
-    def answered(bit, turn):
-        return served(turn) & (pair == 2 * bit - 1)
-
     def ask_copy(index):
         return pltpu.make_async_remote_copy(
-            src_ref=q_hbm.at[:, columns(place(served_turn(index), side))],
+            src_ref=q_hbm.at[:, head_columns((place(served_turn(index), side) + 1) * per_chunk - 1)],
             dst_ref=guest_q.at[index],
             send_sem=ask_send.at[index],
             recv_sem=ask_recv.at[index],
@@ -142,32 +146,41 @@
         )
     pl.semaphore_wait(barrier, len(greeted))
 
-    def unless(condition, action):
-        if condition is False:
-            action()
-        else:
-            pl.when(jnp.logical_not(condition))(action)
+    def for_each_far(turn, action):
+        for bit in range(1, levels):
+            def whole(bit=bit):
+                for part in range(2):
+                    action(block_copy(bit, turn, part, side))
+
+            def less(bit=bit):
+                for part in range(2):
+                    action(block_copy(bit, turn, part, side, per_chunk - 1))
+
+            if serve:
+                pl.when(jnp.logical_not(withheld(bit, turn)))(whole)
+                pl.when(withheld(bit, turn))(less)
+            else:
+                whole()
 
     def send_far(turn):
-        for bit in range(1, levels):
-            def start(bit=bit):
-                for part in range(2):
-                    block_copy(bit, turn, part, side).start()
-
-            unless(withheld(bit, turn) if serve else False, start)
+        for_each_far(turn, lambda copy: copy.start())
 
     def send_near(turn, _):
         for part in range(2):
             block_copy(0, turn, part, 1 - side).start()
         return 0
 
+    def sent_by(turn):
+        more = jnp.maximum(turn - delay(pair) - calm, 0)
+        return jnp.minimum(window + turn + 1 + more, chunks)
+
     if serve:
         @pl.when(lax.rem(pair, 2) == 1)
         def _():
             for index in range(serve):
                 ask_copy(index).start()
 
-    lax.fori_loop(0, min(window, chunks), lambda turn, _: (send_far(turn), 0)[1], 0)
+    lax.fori_loop(0, sent_by(-1), lambda turn, _: (send_far(turn), 0)[1], 0)
     lax.fori_loop(0, chunks, send_near, 0)
 
     row_ids = lax.broadcasted_iota(jnp.int32, (rows, rows), 0)
@@ -178,9 +191,6 @@
     for load in loads:
         load.wait()
     lengths = [len_ref[me]] + [len_ref[partner] for partner in partners]
-
-    def head_columns(head):
-        return pl.ds(pl.multiple_of(head * width, width), width)
 
     def key_value_sum(keys, values, length):
         mapped = jnp.where(live_rows < length, feature(keys.astype(jnp.float32)), 0.0)
@@ -224,23 +234,22 @@
             for cut in cuts
         ]
         if asked:
+            full, cut_short = jnp.where(pair == 1, 2, 1), jnp.where(pair == 1, 1, 2)
+            sources = [
+                (full, jnp.where(pair == 1, lengths[3], lengths[2]), per_chunk),
+                (cut_short, jnp.where(pair == 1, lengths[2], lengths[3]), per_chunk - 1),
+            ]
             index = served_index(turn)
             for copy in answer_copies(index):
                 copy.wait_recv()
             columns_of = jnp.tile(stats_in[index], (rows // 8, 1)).T
-            for offset, found in enumerate(pieces):
-                part = served_in[index, :, offset * width:(offset + 1) * width].astype(jnp.float32)
-                at = 2 * offset
-                found.append((part, columns_of[:, at:at + 1], columns_of[:, at + 1:at + 2]))
-            remaining = [jnp.where(pair == 1, 2, 1)]
-            extents = [jnp.where(pair == 1, lengths[3], lengths[2])]
+            pieces[-1].append((served_in[index].astype(jnp.float32), columns_of[:, :1], columns_of[:, 1:2]))
         else:
-            remaining = range(1, levels)
-            extents = lengths[2:]
-        for bit, extent in zip(remaining, extents):
+            sources = [(bit, lengths[1 + bit], per_chunk) for bit in range(1, levels)]
+        for bit, extent, count in sources:
             for part in range(2):
-                block_copy(bit, turn, part, side).wait_recv()
-            for cut, found in zip(cuts, pieces):
+                block_copy(bit, turn, part, side, count).wait_recv()
+            for cut, found in list(zip(cuts, pieces))[:count]:
                 found.append(piece(q_ref[:, cut], far[bit, 0, :, cut], far[bit, 1, :, cut], extent, False))
         for cut, found in zip(cuts, pieces):
             attention = merge(found)
@@ -251,17 +260,10 @@
 
     def answer(index):
         ask_copy(index).wait_recv()
-        chunk = place(served_turn(index), side)
-        lanes = jnp.zeros((rows, rows), jnp.float32)
-        for offset in range(per_chunk):
-            cut = head_columns(chunk * per_chunk + offset)
-            local = slice(offset * width, (offset + 1) * width)
-            numerator, peak, total = piece(
-                guest_q[index, :, local], k_ref[:, cut], v_ref[:, cut], lengths[0], False
-            )
-            served_out[index, :, local] = numerator.astype(jnp.bfloat16)
-            lanes = jnp.where(column_ids == 2 * offset, peak, lanes)
-            lanes = jnp.where(column_ids == 2 * offset + 1, total, lanes)
+        cut = head_columns((place(served_turn(index), side) + 1) * per_chunk - 1)
+        numerator, peak, total = piece(guest_q[index], k_ref[:, cut], v_ref[:, cut], lengths[0], False)
+        served_out[index] = numerator.astype(jnp.bfloat16)
+        lanes = jnp.where(column_ids == 0, peak, total)
         stats_out[index] = lanes.T[:8]
         for copy in answer_copies(index):
             copy.start()
@@ -283,73 +285,91 @@
         else:
             acc[:, cut] = linear
 
-    def one_turn(turn, _):
-        @pl.when(turn < chunks)
-        def _():
-            chunk = place(turn, side)
-            for part in range(2):
-                block_copy(0, turn, part, side).wait_recv()
+    def prepare(step):
+        for part in range(2):
+            block_copy(0, step, part, side).wait_recv()
+        chunk = place(step, side)
+
+        @pl.when((step < half) | (side > 0))
+        def _():
             for offset in range(per_chunk):
                 head = chunk * per_chunk + offset
                 cut = head_columns(head)
                 near_sums[head] = key_value_sum(far[0, 0, :, cut], far[0, 1, :, cut], lengths[1])
 
-            @pl.when(turn < half)
+        @pl.when((step < half) & (pair < pairs - 1))
+        def _():
+            for offset in range(per_chunk):
+                cut = head_columns(chunk * per_chunk + offset)
+                own_sums[step * per_chunk + offset] = key_value_sum(k_ref[:, cut], v_ref[:, cut], lengths[0])
+
+    def pass_on(link):
+        first = place(link, side) * per_chunk
+
+        @pl.when(pair > 0)
+        def _():
+            chain_copy(link).wait_recv()
+
+        @pl.when(pair < pairs - 1)
+        def _():
+            for offset in range(per_chunk):
+                both = own_sums[link * per_chunk + offset] + near_sums[first + offset]
+                before = jnp.where(pair > 0, chain_in[link, offset].astype(jnp.float32), 0.0)
+                chain_out[link, offset] = (both + before).astype(jnp.bfloat16)
+            chain_copy(link).start()
+
+        @pl.when(pair > 0)
+        def _():
+            swap_copy(link).start()
+
+    def finish_linear(late):
+        @pl.when(pair > 0)
+        def _():
+            swap_copy(late).wait_recv()
+
+        for offset in range(per_chunk):
+            add_linear(place(late, side) * per_chunk + offset, chain_in[late, offset], True)
+
+        def other(finishing):
+            for offset in range(per_chunk):
+                add_linear(place(late, 1 - side) * per_chunk + offset, swap_in[late, offset], finishing)
+
+        if joined:
+            pl.when(late < half - 1)(lambda: other(True))
+            pl.when(late == half - 1)(lambda: other(False))
+        else:
+            other(True)
+
+    def steps(first, limit, action):
+        for offset in range(STEPS):
+            step = first * STEPS + offset
+            pl.when((step >= 0) & (step < limit))(functools.partial(action, step))
+
+    def one_turn(turn, _):
+        steps(turn, chunks, prepare)
+        steps(turn - delay(pair), half, pass_on)
+        lax.fori_loop(sent_by(turn - 1), sent_by(turn), lambda chunk, _: (send_far(chunk), 0)[1], 0)
+        steps(turn - linear_lag, half, finish_linear)
+
+        if serve:
+            @pl.when((pair < pairs // 2) & (turn > 0) & (turn <= serve))
             def _():
-                for offset in range(per_chunk):
-                    cut = head_columns(chunk * per_chunk + offset)
-                    own_sums[turn * per_chunk + offset] = key_value_sum(
-                        k_ref[:, cut], v_ref[:, cut], lengths[0]
-                    )
-
-        link = turn - delay(pair)
-
-        @pl.when((link >= 0) & (link < half))
-        def _():
-            first = place(link, side) * per_chunk
-
-            @pl.when(pair > 0)
-            def _():
-                chain_copy(link).wait_recv()
-                swap_copy(link).start()
-
-            @pl.when(pair < pairs - 1)
-            def _():
-                for offset in range(per_chunk):
-                    both = own_sums[link * per_chunk + offset] + near_sums[first + offset]
-                    before = jnp.where(pair > 0, chain_in[link, offset].astype(jnp.float32), 0.0)
-                    chain_out[link, offset] = (both + before).astype(jnp.bfloat16)
-                chain_copy(link).start()
-
-        @pl.when(turn + window < chunks)
-        def _():
-            send_far(turn + window)
-
-        late = turn - linear_lag
-
-        @pl.when((late >= 0) & (late < half))
-        def _():
-            @pl.when(pair > 0)
-            def _():
-                swap_copy(late).wait_recv()
-
-            for offset in range(per_chunk):
-                add_linear(place(late, side) * per_chunk + offset, chain_in[late, offset], True)
-                add_linear(place(late, 1 - side) * per_chunk + offset, swap_in[late, offset], not linear_first)
-
+                answer(turn - 1)
+
+        asking = served(turn) & (lax.rem(pair, 2) == 1)
+        inside = turn < (chunks - 1 if joined else chunks)
         if serve:
-            @pl.when((pair < pairs // 2) & (lax.rem(turn, 2) == 1) & (turn // 2 < serve))
-            def _():
-                answer(turn // 2)
-
-        asking = served(turn) & (lax.rem(pair, 2) == 1)
-        second = (turn >= half) & (turn < chunks)
-        pl.when(turn < half)(lambda: attend(turn, False, False))
-        if serve:
-            pl.when(second & jnp.logical_not(asking))(lambda: attend(turn, linear_first, False))
-            pl.when(second & asking)(lambda: attend(turn, linear_first, True))
+            pl.when(inside & jnp.logical_not(asking))(lambda: attend(turn, False, False))
+            pl.when(inside & asking)(lambda: attend(turn, False, True))
         else:
-            pl.when(second)(lambda: attend(turn, linear_first, False))
+            pl.when(inside)(lambda: attend(turn, False, False))
+        if joined:
+            last = turn == chunks - 1
+            if serve:
+                pl.when(last & jnp.logical_not(asking))(lambda: attend(turn, True, False))
+                pl.when(last & asking)(lambda: attend(turn, True, True))
+            else:
+                pl.when(last)(lambda: attend(turn, True, False))
 
         return 0
 
@@ -367,12 +387,7 @@
     def finish(turn, _):
         for part in range(2):
             block_copy(0, turn, part, 1 - side).wait_send()
-        for bit in range(1, levels):
-            def wait(bit=bit):
-                for part in range(2):
-                    block_copy(bit, turn, part, side).wait_send()
-
-            unless(withheld(bit, turn) if serve else False, wait)
+        for_each_far(turn, lambda copy: copy.wait_send())
         return 0
 
     lax.fori_loop(0, chunks, finish, 0)
@@ -416,15 +431,14 @@
     levels = blocks.bit_length() - 1
     chunks = heads // HEADS_PER_CHUNK
     half = chunks // 2
-    serve = half // 2 if blocks == 8 else 0
+    serve = SERVED if blocks == 8 else 0
     guests = max(serve, 1)
-    span = HEADS_PER_CHUNK * width
     vmem = pl.BlockSpec(memory_space=pltpu.VMEM)
     hbm = pl.BlockSpec(memory_space=pltpu.HBM)
     piece = (half, HEADS_PER_CHUNK, width, width)
     dma = pltpu.SemaphoreType.DMA
     return pl.pallas_call(
-        functools.partial(kernel, blocks, heads, width, HEADS_PER_CHUNK, WINDOW, delay, serve),
+        functools.partial(kernel, blocks, heads, width, HEADS_PER_CHUNK, WINDOW, CALM, delay, serve),
         out_shape=jax.ShapeDtypeStruct((rows, total), query_rows.dtype),
         in_specs=[hbm, hbm, hbm, hbm, hbm],
         out_specs=vmem,
@@ -448,9 +462,9 @@
             dma((half,)),
             dma((half,)),
             dma((half,)),
-            pltpu.VMEM((guests, rows, span), jnp.bfloat16),
-            pltpu.VMEM((guests, rows, span), jnp.bfloat16),
-            pltpu.VMEM((guests, rows, span), jnp.bfloat16),
+            pltpu.VMEM((guests, rows, width), jnp.bfloat16),
+            pltpu.VMEM((guests, rows, width), jnp.bfloat16),
+            pltpu.VMEM((guests, rows, width), jnp.bfloat16),
             pltpu.VMEM((guests, 8, rows), jnp.float32),
             pltpu.VMEM((guests, 8, rows), jnp.float32),
             dma((guests,)),

time: 82.4 us -> 81.6 us (level)
  no operation moved by 1% of the time
where the time goes in v3:
time: 81.6 us; the launch traced here: 81.4 us
  Pallas kernels  80.5 us (99%)
  local copies, waits for them, and re-layouts  0.88 us (1%)
    pallas_call x1, Pallas kernels, shards(): pl.pallas_call(functools.partial(kernel, blocks, heads, width, HEADS_PER_...  80.5 us

profile of v3, /device:TPU:0, one launch (start us, length us, event | category | flops | bytes accessed | tf_op | source)
XLA Modules:
  0.0 81.4 jit_solution(4632716449740164481)
XLA Ops:
  0.0 80.5 %butterfly.1 = bf16[128,3072]{1,0:T(8,128)(2,1)S(1)} custom-call(s32[8]{0:T(128)} %len_hbm.1, f32[24]{0:T(128)} %scale_hbm.1, bf16[128,3072]{1,0:T(8,128)(2,1)} %q_hbm.1, bf16[128,3072]{1,0:T(8,128)(2,1)} %k_hbm.1, bf16[128,3072]{1,0:T(8,128)(2,1)} %v_hbm.1), custom_call_target="tpu_custom_call" | custom-call | tf_op jit(solution)/shard_map/butterfly/pallas_call | solution.py:440
  80.5 0.9 %copy.7 = bf16[128,3072]{1,0:T(8,128)(2,1)} copy(bf16[128,3072]{1,0:T(8,128)(2,1)S(1)} %butterfly.1) | data formatting | bytes 1572864

commit v4 on v3

--- a/solution.py
+++ b/solution.py
@@ -147,6 +147,12 @@
     pl.semaphore_wait(barrier, len(greeted))
 
     def for_each_far(turn, action):
+        if serve:
+            for part in range(2):
+                for bit in range(1, levels):
+                    pl.when(jnp.logical_not(withheld(bit, turn)))(lambda bit=bit: action(block_copy(bit, turn, part, side)))
+                    pl.when(withheld(bit, turn))(lambda bit=bit: action(block_copy(bit, turn, part, side, per_chunk - 1)))
+            return
         for bit in range(1, levels):
             def whole(bit=bit):
                 for part in range(2):
@@ -202,6 +208,10 @@
         )
 
     def piece(queries, keys, values, length, causal):
+        weights, peak, total = weigh(queries, keys, length, causal)
+        return jnp.dot(weights, values, preferred_element_type=jnp.float32), peak, total
+
+    def weigh(queries, keys, length, causal):
         scores = root * lax.dot_general(
             queries, keys, (((1,), (1,)), ((), ())), preferred_element_type=jnp.float32
         )
@@ -211,8 +221,7 @@
         peak = jnp.max(jnp.where(allowed, scores, -jnp.inf), axis=1, keepdims=True)
         weights = jnp.where(allowed, jnp.exp(scores - peak), 0.0).astype(jnp.bfloat16)
         total = jnp.sum(weights.astype(jnp.float32), axis=1, keepdims=True)
-        numerator = jnp.dot(weights, values, preferred_element_type=jnp.float32)
-        return numerator, peak, total
+        return weights, peak, total
 
     def merge(pieces):
         top = functools.reduce(jnp.maximum, [peak for _, peak, _ in pieces])
@@ -246,11 +255,15 @@
             pieces[-1].append((served_in[index].astype(jnp.float32), columns_of[:, :1], columns_of[:, 1:2]))
         else:
             sources = [(bit, lengths[1 + bit], per_chunk) for bit in range(1, levels)]
+        heavy = []
         for bit, extent, count in sources:
-            for part in range(2):
-                block_copy(bit, turn, part, side, count).wait_recv()
-            for cut, found in list(zip(cuts, pieces))[:count]:
-                found.append(piece(q_ref[:, cut], far[bit, 0, :, cut], far[bit, 1, :, cut], extent, False))
+            block_copy(bit, turn, 0, side, count).wait_recv()
+            heavy.append([weigh(q_ref[:, cut], far[bit, 0, :, cut], extent, False) for cut in cuts[:count]])
+        for (bit, extent, count), weighed in zip(sources, heavy):
+            block_copy(bit, turn, 1, side, count).wait_recv()
+            for cut, found, (weights, peak, total) in zip(cuts, pieces, weighed):
+                numerator = jnp.dot(weights, far[bit, 1, :, cut], preferred_element_type=jnp.float32)
+                found.append((numerator, peak, total))
         for cut, found in zip(cuts, pieces):
             attention = merge(found)
             if finishing:

time: 81.6 us -> 81.2 us (level)
  no operation moved by 1% of the time
where the time goes in v4:
time: 81.2 us; the launch traced here: 81.1 us
  Pallas kernels  80.2 us (99%)
  local copies, waits for them, and re-layouts  0.88 us (1%)
    pallas_call x1, Pallas kernels, shards(): pl.pallas_call(functools.partial(kernel, blocks, heads, width, HEADS_PER_...  80.2 us

profile of v4, /device:TPU:0, one launch (start us, length us, event | category | flops | bytes accessed | tf_op | source)
XLA Modules:
  0.0 81.1 jit_solution(7010390831236982735)
XLA Ops:
  0.0 80.2 %butterfly.1 = bf16[128,3072]{1,0:T(8,128)(2,1)S(1)} custom-call(s32[8]{0:T(128)} %len_hbm.1, f32[24]{0:T(128)} %scale_hbm.1, bf16[128,3072]{1,0:T(8,128)(2,1)} %q_hbm.1, bf16[128,3072]{1,0:T(8,128)(2,1)} %k_hbm.1, bf16[128,3072]{1,0:T(8,128)(2,1)} %v_hbm.1), custom_call_target="tpu_custom_call" | custom-call | tf_op jit(solution)/shard_map/butterfly/pallas_call | solution.py:453
  80.2 0.9 %copy.7 = bf16[128,3072]{1,0:T(8,128)(2,1)} copy(bf16[128,3072]{1,0:T(8,128)(2,1)S(1)} %butterfly.1) | data formatting | bytes 1572864

commit v5 on v4

--- a/solution.py
+++ b/solution.py
@@ -30,7 +30,7 @@
     blocks, heads, width, per_chunk, window, calm, delay, serve,
     len_hbm, scale_hbm, q_hbm, k_hbm, v_hbm, out_ref,
     len_ref, scale_ref, q_ref, k_ref, v_ref, load_sem, far, acc, own_sums, near_sums, chain_out, chain_in, swap_in,
-    send_sem, recv_sem, chain_send, chain_recv, swap_send, swap_recv,
+    send_sem, recv_sem, near_recv, chain_send, chain_recv, swap_send, swap_recv,
     guest_q, served_out, served_in, stats_out, stats_in, ask_send, ask_recv, answer_send, answer_recv,
 ):
     rows = q_ref.shape[0]
@@ -39,7 +39,8 @@
     half = chunks // 2
     pairs = blocks // 2
     span = per_chunk * width
-    rounds = pl.cdiv(half, STEPS)
+    step_count = STEPS if half % STEPS == 0 else 1
+    rounds = half // step_count
     linear_lag = max(chunks - rounds, delay(pairs - 1) + 1)
     joined = linear_lag + rounds == chunks
     turns = linear_lag + rounds
@@ -60,34 +61,69 @@
     def head_columns(head):
         return pl.ds(pl.multiple_of(head * width, width), width)
 
+    def slot(turn, part):
+        return jnp.where(turn == chunks - 1, chunks, turn) if joined and part else turn
+
+    def arrival(place_in_far, received):
+        return pltpu.make_async_remote_copy(
+            src_ref=place_in_far,
+            dst_ref=place_in_far,
+            send_sem=send_sem.at[0, 0],
+            recv_sem=received,
+            device_id={"seq": partners[0]},
+            device_id_type=pl.DeviceIdType.MESH,
+        )
+
+    def near_arrival(group):
+        start = place(group * step_count, side) * span
+        cut = pl.ds(pl.multiple_of(start, span), step_count * span)
+        return arrival(far.at[0, :, :, cut], near_recv.at[group])
+
+    def far_arrival(bit, turn, count):
+        cut = pl.ds(pl.multiple_of(place(turn, side) * span, span), count * width)
+        return arrival(far.at[bit, :, :, cut], recv_sem.at[bit - 1, turn])
+
+    def departure(source, sent):
+        return pltpu.make_async_remote_copy(
+            src_ref=source,
+            dst_ref=source,
+            send_sem=sent,
+            recv_sem=near_recv.at[0],
+            device_id={"seq": partners[0]},
+            device_id_type=pl.DeviceIdType.MESH,
+        )
+
     def block_copy(bit, turn, part, which, heads_sent=per_chunk):
         source = k_hbm if part == 0 else v_hbm
         cut = pl.ds(pl.multiple_of(place(turn, which) * span, span), heads_sent * width)
         return pltpu.make_async_remote_copy(
             src_ref=source.at[:, cut],
             dst_ref=far.at[bit, part, :, cut],
-            send_sem=send_sem.at[bit, turn, part],
-            recv_sem=recv_sem.at[bit, turn, part],
+            send_sem=send_sem.at[bit, part],
+            recv_sem=near_recv.at[turn // step_count] if isinstance(bit, int) and bit == 0 else recv_sem.at[bit - 1, slot(turn, part)],
             device_id={"seq": partners[bit] if isinstance(bit, int) else partners[1]},
             device_id_type=pl.DeviceIdType.MESH,
         )
 
-    def chain_copy(turn):
+    def in_round(number):
+        return pl.ds(number * step_count, step_count)
+
+    def chain_copy(number):
         return pltpu.make_async_remote_copy(
-            src_ref=chain_out.at[turn],
-            dst_ref=chain_in.at[turn],
-            send_sem=chain_send.at[turn],
-            recv_sem=chain_recv.at[turn],
+            src_ref=chain_out.at[in_round(number)],
+            dst_ref=chain_in.at[in_round(number)],
+            send_sem=chain_send.at[0],
+            recv_sem=chain_recv.at[number],
             device_id={"seq": above},
             device_id_type=pl.DeviceIdType.MESH,
         )
 
-    def swap_copy(turn):
+    def swap_copy(number):
         return pltpu.make_async_remote_copy(
-            src_ref=chain_in.at[turn],
-            dst_ref=swap_in.at[turn],
-            send_sem=swap_send.at[turn],
-            recv_sem=swap_recv.at[turn],
+            src_ref=chain_in.at[in_round(number)],
+            dst_ref=swap_in.at[in_round(number)],
+            send_sem=swap_send.at[0],
+            recv_sem=swap_recv.at[number],
             device_id={"seq": partners[0]},
             device_id_type=pl.DeviceIdType.MESH,
         )
@@ -111,8 +147,8 @@
         return pltpu.make_async_remote_copy(
             src_ref=q_hbm.at[:, head_columns((place(served_turn(index), side) + 1) * per_chunk - 1)],
             dst_ref=guest_q.at[index],
-            send_sem=ask_send.at[index],
-            recv_sem=ask_recv.at[index],
+            send_sem=ask_send.at[0],
+            recv_sem=ask_recv.at[0],
             device_id={"seq": host},
             device_id_type=pl.DeviceIdType.MESH,
         )
@@ -122,7 +158,7 @@
             pltpu.make_async_remote_copy(
                 src_ref=source.at[index],
                 dst_ref=target.at[index],
-                send_sem=answer_send.at[index, part],
+                send_sem=answer_send.at[part],
                 recv_sem=answer_recv.at[index, part],
                 device_id={"seq": guest},
                 device_id_type=pl.DeviceIdType.MESH,
@@ -136,14 +172,14 @@
             ((k_hbm, k_ref), (v_hbm, v_ref), (q_hbm, q_ref), (len_hbm, len_ref), (scale_hbm, scale_ref))
         )
     ]
-    for load in loads:
-        load.start()
     barrier = pltpu.get_barrier_semaphore()
     greeted = partners + [above, below]
     for other in greeted:
         pl.semaphore_signal(
             barrier, inc=1, device_id={"seq": other}, device_id_type=pl.DeviceIdType.MESH
         )
+    for load in loads:
+        load.start()
     pl.semaphore_wait(barrier, len(greeted))
 
     def for_each_far(turn, action):
@@ -255,15 +291,21 @@
             pieces[-1].append((served_in[index].astype(jnp.float32), columns_of[:, :1], columns_of[:, 1:2]))
         else:
             sources = [(bit, lengths[1 + bit], per_chunk) for bit in range(1, levels)]
-        heavy = []
-        for bit, extent, count in sources:
-            block_copy(bit, turn, 0, side, count).wait_recv()
-            heavy.append([weigh(q_ref[:, cut], far[bit, 0, :, cut], extent, False) for cut in cuts[:count]])
-        for (bit, extent, count), weighed in zip(sources, heavy):
-            block_copy(bit, turn, 1, side, count).wait_recv()
-            for cut, found, (weights, peak, total) in zip(cuts, pieces, weighed):
-                numerator = jnp.dot(weights, far[bit, 1, :, cut], preferred_element_type=jnp.float32)
-                found.append((numerator, peak, total))
+        if finishing:
+            heavy = []
+            for bit, extent, count in sources:
+                block_copy(bit, turn, 0, side, count).wait_recv()
+                heavy.append([weigh(q_ref[:, cut], far[bit, 0, :, cut], extent, False) for cut in cuts[:count]])
+            for (bit, extent, count), weighed in zip(sources, heavy):
+                block_copy(bit, turn, 1, side, count).wait_recv()
+                for cut, found, (weights, peak, total) in zip(cuts, pieces, weighed):
+                    numerator = jnp.dot(weights, far[bit, 1, :, cut], preferred_element_type=jnp.float32)
+                    found.append((numerator, peak, total))
+        else:
+            for bit, extent, count in sources:
+                far_arrival(bit, turn, count).wait_recv()
+                for cut, found in list(zip(cuts, pieces))[:count]:
+                    found.append(piece(q_ref[:, cut], far[bit, 0, :, cut], far[bit, 1, :, cut], extent, False))
         for cut, found in zip(cuts, pieces):
             attention = merge(found)
             if finishing:
@@ -272,7 +314,10 @@
                 acc[:, cut] = attention
 
     def answer(index):
-        ask_copy(index).wait_recv()
+        @pl.when(index == 0)
+        def _():
+            arrival(guest_q, ask_recv.at[0]).wait_recv()
+
         cut = head_columns((place(served_turn(index), side) + 1) * per_chunk - 1)
         numerator, peak, total = piece(guest_q[index], k_ref[:, cut], v_ref[:, cut], lengths[0], False)
         served_out[index] = numerator.astype(jnp.bfloat16)
@@ -299,8 +344,6 @@
             acc[:, cut] = linear
 
     def prepare(step):
-        for part in range(2):
-            block_copy(0, step, part, side).wait_recv()
         chunk = place(step, side)
 
         @pl.when((step < half) | (side > 0))
@@ -316,30 +359,40 @@
                 cut = head_columns(chunk * per_chunk + offset)
                 own_sums[step * per_chunk + offset] = key_value_sum(k_ref[:, cut], v_ref[:, cut], lengths[0])
 
-    def pass_on(link):
-        first = place(link, side) * per_chunk
-
+    def prepare_group(group):
+        near_arrival(group).wait_recv()
+        for offset in range(step_count):
+            prepare(group * step_count + offset)
+
+    def pass_on(number):
         @pl.when(pair > 0)
         def _():
-            chain_copy(link).wait_recv()
+            chain_copy(number).wait_recv()
 
         @pl.when(pair < pairs - 1)
         def _():
-            for offset in range(per_chunk):
-                both = own_sums[link * per_chunk + offset] + near_sums[first + offset]
-                before = jnp.where(pair > 0, chain_in[link, offset].astype(jnp.float32), 0.0)
-                chain_out[link, offset] = (both + before).astype(jnp.bfloat16)
-            chain_copy(link).start()
+            for part in range(step_count):
+                link = number * step_count + part
+                first = place(link, side) * per_chunk
+                for offset in range(per_chunk):
+                    both = own_sums[link * per_chunk + offset] + near_sums[first + offset]
+                    before = jnp.where(pair > 0, chain_in[link, offset].astype(jnp.float32), 0.0)
+                    chain_out[link, offset] = (both + before).astype(jnp.bfloat16)
+            chain_copy(number).start()
 
         @pl.when(pair > 0)
         def _():
-            swap_copy(link).start()
+            swap_copy(number).start()
+
+    def linear_round(number):
+        @pl.when(pair > 0)
+        def _():
+            swap_copy(number).wait_recv()
+
+        for part in range(step_count):
+            finish_linear(number * step_count + part)
 
     def finish_linear(late):
-        @pl.when(pair > 0)
-        def _():
-            swap_copy(late).wait_recv()
-
         for offset in range(per_chunk):
             add_linear(place(late, side) * per_chunk + offset, chain_in[late, offset], True)
 
@@ -353,16 +406,12 @@
         else:
             other(True)
 
-    def steps(first, limit, action):
-        for offset in range(STEPS):
-            step = first * STEPS + offset
-            pl.when((step >= 0) & (step < limit))(functools.partial(action, step))
-
     def one_turn(turn, _):
-        steps(turn, chunks, prepare)
-        steps(turn - delay(pair), half, pass_on)
+        pl.when(turn < chunks // step_count)(lambda: prepare_group(turn))
+        number = turn - delay(pair)
+        pl.when((number >= 0) & (number < rounds))(lambda: pass_on(number))
         lax.fori_loop(sent_by(turn - 1), sent_by(turn), lambda chunk, _: (send_far(chunk), 0)[1], 0)
-        steps(turn - linear_lag, half, finish_linear)
+        pl.when((turn >= linear_lag) & (turn - linear_lag < rounds))(lambda: linear_round(turn - linear_lag))
 
         if serve:
             @pl.when((pair < pairs // 2) & (turn > 0) & (turn <= serve))
@@ -397,40 +446,28 @@
 
     lax.fori_loop(0, turns, one_turn, 0)
 
-    def finish(turn, _):
-        for part in range(2):
-            block_copy(0, turn, part, 1 - side).wait_send()
-        for_each_far(turn, lambda copy: copy.wait_send())
-        return 0
-
-    lax.fori_loop(0, chunks, finish, 0)
-
-    def finish_chain(turn, _):
-        @pl.when(pair < pairs - 1)
-        def _():
-            chain_copy(turn).wait_send()
-
-        @pl.when(pair > 0)
-        def _():
-            swap_copy(turn).wait_send()
-
-        return 0
-
-    lax.fori_loop(0, half, finish_chain, 0)
-
-    def finish_served(index, _):
+    for part, source in enumerate((k_hbm, v_hbm)):
+        departure(source, send_sem.at[0, part]).wait_send()
+        for bit in range(1, levels):
+            if serve:
+                pl.when(pair != bit - 1)(departure(source, send_sem.at[bit, part]).wait_send)
+                some = source.at[:, :(heads - serve) * width]
+                pl.when(pair == bit - 1)(departure(some, send_sem.at[bit, part]).wait_send)
+            else:
+                departure(source, send_sem.at[bit, part]).wait_send()
+
+    pl.when(pair < pairs - 1)(departure(chain_out, chain_send.at[0]).wait_send)
+    pl.when(pair > 0)(departure(chain_in, swap_send.at[0]).wait_send)
+
+    if serve:
         @pl.when(lax.rem(pair, 2) == 1)
         def _():
-            ask_copy(index).wait_send()
+            departure(guest_q, ask_send.at[0]).wait_send()
 
         @pl.when(pair < pairs // 2)
         def _():
-            for copy in answer_copies(index):
-                copy.wait_send()
-
-        return 0
-
-    lax.fori_loop(0, serve, finish_served, 0)
+            departure(served_out, answer_send.at[0]).wait_send()
+            departure(stats_out, answer_send.at[1]).wait_send()
 
 
 def delay(pair):
@@ -444,6 +481,7 @@
     levels = blocks.bit_length() - 1
     chunks = heads // HEADS_PER_CHUNK
     half = chunks // 2
+    step_count = STEPS if half % STEPS == 0 else 1
     serve = SERVED if blocks == 8 else 0
     guests = max(serve, 1)
     vmem = pl.BlockSpec(memory_space=pltpu.VMEM)
@@ -469,20 +507,21 @@
             pltpu.VMEM(piece, jnp.bfloat16),
             pltpu.VMEM(piece, jnp.bfloat16),
             pltpu.VMEM(piece, jnp.bfloat16),
-            dma((levels, chunks, 2)),
-            dma((levels, chunks, 2)),
-            dma((half,)),
-            dma((half,)),
-            dma((half,)),
-            dma((half,)),
+            dma((levels, 2)),
+            dma((levels - 1, chunks + 1)),
+            dma((chunks // step_count,)),
+            dma((1,)),
+            dma((half // step_count,)),
+            dma((1,)),
+            dma((half // step_count,)),
             pltpu.VMEM((guests, rows, width), jnp.bfloat16),
             pltpu.VMEM((guests, rows, width), jnp.bfloat16),
             pltpu.VMEM((guests, rows, width), jnp.bfloat16),
             pltpu.VMEM((guests, 8, rows), jnp.float32),
             pltpu.VMEM((guests, 8, rows), jnp.float32),
-            dma((guests,)),
-            dma((guests,)),
-            dma((guests, 2)),
+            dma((1,)),
+            dma((1,)),
+            dma((2,)),
             dma((guests, 2)),
         ],
         compiler_params=pltpu.CompilerParams(

time: 81.2 us -> 80.3 us (0.989)
  Pallas kernels: 80.2 us -> 79 us
    pallas_call x1, Pallas kernels: 80.2 us -> 79 us  [shards(): pl.pallas_call(functools.partial(kernel, blocks, heads, width, HEADS_PER_...]
where the time goes in v5:
time: 80.3 us; the launch traced here: 79.9 us
  Pallas kernels  79 us (98%)
  local copies, waits for them, and re-layouts  0.88 us (1%)
    pallas_call x1, Pallas kernels, shards(): pl.pallas_call(functools.partial(kernel, blocks, heads, width, HEADS_PER_...  79 us

profile of v5, /device:TPU:0, one launch (start us, length us, event | category | flops | bytes accessed | tf_op | source)
XLA Modules:
  0.0 79.9 jit_solution(13049822489172312814)
XLA Ops:
  0.0 79.0 %butterfly.1 = bf16[128,3072]{1,0:T(8,128)(2,1)S(1)} custom-call(s32[8]{0:T(128)} %len_hbm.1, f32[24]{0:T(128)} %scale_hbm.1, bf16[128,3072]{1,0:T(8,128)(2,1)} %q_hbm.1, bf16[128,3072]{1,0:T(8,128)(2,1)} %k_hbm.1, bf16[128,3072]{1,0:T(8,128)(2,1)} %v_hbm.1), custom_call_target="tpu_custom_call" | custom-call | tf_op jit(solution)/shard_map/butterfly/pallas_call | solution.py:491
  79.0 0.9 %copy.7 = bf16[128,3072]{1,0:T(8,128)(2,1)} copy(bf16[128,3072]{1,0:T(8,128)(2,1)S(1)} %butterfly.1) | data formatting | bytes 1572864

commit v6 on v5

--- a/solution.py
+++ b/solution.py
@@ -9,7 +9,7 @@
 from jax.sharding import PartitionSpec as P
 
 HEADS_PER_CHUNK = 2
-WINDOW = 2
+WINDOW = 3
 STEPS = 2
 CALM = 3
 SERVED = 5
@@ -186,23 +186,13 @@
         if serve:
             for part in range(2):
                 for bit in range(1, levels):
-                    pl.when(jnp.logical_not(withheld(bit, turn)))(lambda bit=bit: action(block_copy(bit, turn, part, side)))
-                    pl.when(withheld(bit, turn))(lambda bit=bit: action(block_copy(bit, turn, part, side, per_chunk - 1)))
+                    less = withheld(bit, turn)
+                    pl.when(jnp.logical_not(less))(lambda: action(block_copy(bit, turn, part, side)))
+                    pl.when(less)(lambda: action(block_copy(bit, turn, part, side, per_chunk - 1)))
             return
-        for bit in range(1, levels):
-            def whole(bit=bit):
-                for part in range(2):
-                    action(block_copy(bit, turn, part, side))
-
-            def less(bit=bit):
-                for part in range(2):
-                    action(block_copy(bit, turn, part, side, per_chunk - 1))
-
-            if serve:
-                pl.when(jnp.logical_not(withheld(bit, turn)))(whole)
-                pl.when(withheld(bit, turn))(less)
-            else:
-                whole()
+        for part in range(2):
+            for bit in range(1, levels):
+                action(block_copy(bit, turn, part, side))
 
     def send_far(turn):
         for_each_far(turn, lambda copy: copy.start())

time: 80.3 us -> 80 us (level)
  no operation moved by 1% of the time
where the time goes in v6:
time: 80 us; the launch traced here: 79.8 us
  Pallas kernels  78.9 us (99%)
  local copies, waits for them, and re-layouts  0.88 us (1%)
    pallas_call x1, Pallas kernels, shards(): pl.pallas_call(functools.partial(kernel, blocks, heads, width, HEADS_PER_...  78.9 us

profile of v6, /device:TPU:0, one launch (start us, length us, event | category | flops | bytes accessed | tf_op | source)
XLA Modules:
  0.0 79.8 jit_solution(4154198329798340923)
XLA Ops:
  0.0 78.9 %butterfly.1 = bf16[128,3072]{1,0:T(8,128)(2,1)S(1)} custom-call(s32[8]{0:T(128)} %len_hbm.1, f32[24]{0:T(128)} %scale_hbm.1, bf16[128,3072]{1,0:T(8,128)(2,1)} %q_hbm.1, bf16[128,3072]{1,0:T(8,128)(2,1)} %k_hbm.1, bf16[128,3072]{1,0:T(8,128)(2,1)} %v_hbm.1), custom_call_target="tpu_custom_call" | custom-call | tf_op jit(solution)/shard_map/butterfly/pallas_call | solution.py:481
  78.9 0.9 %copy.7 = bf16[128,3072]{1,0:T(8,128)(2,1)} copy(bf16[128,3072]{1,0:T(8,128)(2,1)S(1)} %butterfly.1) | data formatting | bytes 1572864

commit v7 on v6

--- a/solution.py
+++ b/solution.py
@@ -173,14 +173,19 @@
         )
     ]
     barrier = pltpu.get_barrier_semaphore()
-    greeted = partners + [above, below]
-    for other in greeted:
+
+    def greet(other):
         pl.semaphore_signal(
             barrier, inc=1, device_id={"seq": other}, device_id_type=pl.DeviceIdType.MESH
         )
+
+    for other in partners:
+        greet(other)
+    pl.when(pair < pairs - 1)(lambda: greet(above))
+    pl.when(pair > 0)(lambda: greet(below))
     for load in loads:
         load.start()
-    pl.semaphore_wait(barrier, len(greeted))
+    pl.semaphore_wait(barrier, len(partners) + jnp.where((pair > 0) & (pair < pairs - 1), 2, 1))
 
     def for_each_far(turn, action):
         if serve:

time: 80 us -> 79.5 us (level)
  no operation moved by 1% of the time
where the time goes in v7:
time: 79.5 us; the launch traced here: 79.4 us
  Pallas kernels  78.5 us (99%)
  local copies, waits for them, and re-layouts  0.88 us (1%)
    pallas_call x1, Pallas kernels, shards(): pl.pallas_call(functools.partial(kernel, blocks, heads, width, HEADS_PER_...  78.5 us

profile of v7, /device:TPU:0, one launch (start us, length us, event | category | flops | bytes accessed | tf_op | source)
XLA Modules:
  0.0 79.4 jit_solution(7531400385258209249)
XLA Ops:
  0.0 78.5 %butterfly.1 = bf16[128,3072]{1,0:T(8,128)(2,1)S(1)} custom-call(s32[8]{0:T(128)} %len_hbm.1, f32[24]{0:T(128)} %scale_hbm.1, bf16[128,3072]{1,0:T(8,128)(2,1)} %q_hbm.1, bf16[128,3072]{1,0:T(8,128)(2,1)} %k_hbm.1, bf16[128,3072]{1,0:T(8,128)(2,1)} %v_hbm.1), custom_call_target="tpu_custom_call" | custom-call | tf_op jit(solution)/shard_map/butterfly/pallas_call | solution.py:486
  78.5 0.9 %copy.7 = bf16[128,3072]{1,0:T(8,128)(2,1)} copy(bf16[128,3072]{1,0:T(8,128)(2,1)S(1)} %butterfly.1) | data formatting | bytes 1572864

commit v8 on v7

--- a/solution.py
+++ b/solution.py
@@ -190,7 +190,7 @@
     def for_each_far(turn, action):
         if serve:
             for part in range(2):
-                for bit in range(1, levels):
+                for bit in reversed(range(1, levels)):
                     less = withheld(bit, turn)
                     pl.when(jnp.logical_not(less))(lambda: action(block_copy(bit, turn, part, side)))
                     pl.when(less)(lambda: action(block_copy(bit, turn, part, side, per_chunk - 1)))

time: 79.5 us -> 79.2 us (level)
  no operation moved by 1% of the time
where the time goes in v8:
time: 79.2 us; the launch traced here: 79 us
  Pallas kernels  78.1 us (99%)
  local copies, waits for them, and re-layouts  0.88 us (1%)
    pallas_call x1, Pallas kernels, shards(): pl.pallas_call(functools.partial(kernel, blocks, heads, width, HEADS_PER_...  78.1 us

profile of v8, /device:TPU:0, one launch (start us, length us, event | category | flops | bytes accessed | tf_op | source)
XLA Modules:
  0.0 79.0 jit_solution(14780503361287628261)
XLA Ops:
  0.0 78.1 %butterfly.1 = bf16[128,3072]{1,0:T(8,128)(2,1)S(1)} custom-call(s32[8]{0:T(128)} %len_hbm.1, f32[24]{0:T(128)} %scale_hbm.1, bf16[128,3072]{1,0:T(8,128)(2,1)} %q_hbm.1, bf16[128,3072]{1,0:T(8,128)(2,1)} %k_hbm.1, bf16[128,3072]{1,0:T(8,128)(2,1)} %v_hbm.1), custom_call_target="tpu_custom_call" | custom-call | tf_op jit(solution)/shard_map/butterfly/pallas_call | solution.py:486
  78.1 0.9 %copy.7 = bf16[128,3072]{1,0:T(8,128)(2,1)} copy(bf16[128,3072]{1,0:T(8,128)(2,1)S(1)} %butterfly.1) | data formatting | bytes 1572864

commit v9 on v8

--- a/solution.py
+++ b/solution.py
@@ -183,8 +183,6 @@
         greet(other)
     pl.when(pair < pairs - 1)(lambda: greet(above))
     pl.when(pair > 0)(lambda: greet(below))
-    for load in loads:
-        load.start()
     pl.semaphore_wait(barrier, len(partners) + jnp.where((pair > 0) & (pair < pairs - 1), 2, 1))
 
     def for_each_far(turn, action):
@@ -204,7 +202,7 @@
 
     def send_near(turn, _):
         for part in range(2):
-            block_copy(0, turn, part, 1 - side).start()
+            block_copy(0, turn * step_count, part, 1 - side, per_chunk * step_count).start()
         return 0
 
     def sent_by(turn):
@@ -218,7 +216,9 @@
                 ask_copy(index).start()
 
     lax.fori_loop(0, sent_by(-1), lambda turn, _: (send_far(turn), 0)[1], 0)
-    lax.fori_loop(0, chunks, send_near, 0)
+    for load in loads:
+        load.start()
+    lax.fori_loop(0, chunks // step_count, send_near, 0)
 
     row_ids = lax.broadcasted_iota(jnp.int32, (rows, rows), 0)
     column_ids = lax.broadcasted_iota(jnp.int32, (rows, rows), 1)

time: 79.2 us -> 79.2 us (level)
  no operation moved by 1% of the time
where the time goes in v9:
time: 79.2 us; the launch traced here: 79 us
  Pallas kernels  78.1 us (99%)
  local copies, waits for them, and re-layouts  0.88 us (1%)
    pallas_call x1, Pallas kernels, shards(): pl.pallas_call(functools.partial(kernel, blocks, heads, width, HEADS_PER_...  78.1 us

profile of v9, /device:TPU:0, one launch (start us, length us, event | category | flops | bytes accessed | tf_op | source)
XLA Modules:
  0.0 79.0 jit_solution(9800045445777327342)
XLA Ops:
  0.0 78.1 %butterfly.1 = bf16[128,3072]{1,0:T(8,128)(2,1)S(1)} custom-call(s32[8]{0:T(128)} %len_hbm.1, f32[24]{0:T(128)} %scale_hbm.1, bf16[128,3072]{1,0:T(8,128)(2,1)} %q_hbm.1, bf16[128,3072]{1,0:T(8,128)(2,1)} %k_hbm.1, bf16[128,3072]{1,0:T(8,128)(2,1)} %v_hbm.1), custom_call_target="tpu_custom_call" | custom-call | tf_op jit(solution)/shard_map/butterfly/pallas_call | solution.py:486
  78.1 0.9 %copy.7 = bf16[128,3072]{1,0:T(8,128)(2,1)} copy(bf16[128,3072]{1,0:T(8,128)(2,1)S(1)} %butterfly.1) | data formatting | bytes 1572864
